TPU v7x, 128 devices: a whole 4x4x4 slice. The times are simulated.
128 devices in a mesh: space: 32 (over z, y, core), mode: 4 (over x).
Axes of the slice: x: 4, y: 4, z: 4, core: 2. Of those that a mesh axis runs over, the one named last changes fastest.
Arguments:
- velocity: float32 [3, 512, 512, 256], P(None, 'space', 'mode'), may hold values from -6 to 6
- basis: float32 [32, 3145728], P('mode', 'space'), may hold values from -42 to 42
- levels: float32 [8], replicated, may hold values from 0.02 to 0.15
- profile_index: int32 [256], replicated, may hold values from 0 to 7
- advect: float32 [256], replicated, may hold values from 0 to 0.4
Outputs:
- modes: float32 [32, 3145728], P('mode', 'space')
- sigma: float32 [32], replicated
Inputs may be any that keep to these rules, and one draw needn't show every extreme that they name: `profile_index`: each entry picks one of the 8 viscosity levels.
All inputs are finite; a program needn't handle non-finite values.
Results may differ from a plain program's by a relative error of at most 0.0055.
Values sent between devices are 32-bit elements; how exact they have to be, the bound alone decides.
No kernel may reach another device: no remote copies, remote signals or barrier semaphores. Data moves between devices by JAX's collectives and lax.ppermute only.
A program may use at most 128 MiB of HBM per device.

v0:
```python
import math
import jax
import jax.numpy as jnp
import numpy as np
from jax import lax
from jax.sharding import PartitionSpec as P

STRIDE = 4
MODES = 32
SWEEPS = 2


def extended(x, sides, width):
    for axis, dim in sides:
        size, length = (lax.axis_size(axis), x.shape[dim])
        up = [(i, (i + 1) % size) for i in range(size)]
        down = [(j, i) for i, j in up]
        last = lax.slice_in_dim(x, length - width, length, axis=dim)
        leading = lax.slice_in_dim(x, 0, width, axis=dim)
        before = lax.ppermute(last, axis, up)
        after = lax.ppermute(leading, axis, down)
        x = jnp.concatenate([before, x, after], axis=dim)
    return x


def profile(levels, profile_index):
    table = (
        profile_index[:, None] == jnp.arange(levels.shape[0], dtype=jnp.int32)[None, :]
    ).astype(jnp.float32)
    viscosity = jnp.sum(table * levels[None, :], axis=1)
    middle = 0.5 * (viscosity[:-1] + viscosity[1:])
    face_up = jnp.concatenate([middle, viscosity[-1:]])
    face_down = jnp.concatenate([viscosity[:1], middle])
    return (viscosity, face_down, face_up)


def advance(field, viscosity, face_down, face_up, advect):
    center = field[:, 1:-1, 1:-1, :]
    east = field[:, 2:, 1:-1, :]
    west = field[:, :-2, 1:-1, :]
    north = field[:, 1:-1, 2:, :]
    south = field[:, 1:-1, :-2, :]
    walled = jnp.pad(center, ((0, 0), (0, 0), (0, 0), (1, 1)))
    upward = walled[..., 2:]
    downward = walled[..., :-2]
    lateral = east + west + north + south - 4.0 * center
    vertical = face_up * (upward - center) - face_down * (center - downward)
    return center + viscosity * lateral + vertical - 0.5 * advect * (east - west)


def coarsen(field):
    components, x_cells, z_cells, y_cells = field.shape
    plane = z_cells * y_cells
    slabs = field.reshape(components * (x_cells // STRIDE), STRIDE * plane)
    along_x = slabs[:, 0:plane]
    for offset in range(1, STRIDE):
        along_x = along_x + slabs[:, offset * plane : (offset + 1) * plane]
    lines = along_x.reshape(
        components * (x_cells // STRIDE) * (z_cells // STRIDE), STRIDE * y_cells
    )
    along_z = lines[:, 0:y_cells]
    for offset in range(1, STRIDE):
        along_z = along_z + lines[:, offset * y_cells : (offset + 1) * y_cells]
    cell_ids = jnp.arange(y_cells, dtype=jnp.int32)[:, None] // STRIDE
    box_ids = jnp.arange(y_cells // STRIDE, dtype=jnp.int32)[None, :]
    summing = (cell_ids == box_ids).astype(jnp.float32)
    boxed = jnp.dot(
        along_z, summing, precision=lax.Precision.HIGHEST, preferred_element_type=jnp.float32
    )
    return (boxed / math.sqrt(STRIDE**3)).reshape(-1)


def with_faces(field):
    return extended(field, (("space", 1), ("mode", 2)), 1)


def round_order(count, turn):
    players = [0] + [1 + (i_pos - 1 + turn) % (count - 1) for i_pos in range(1, count)]
    leading = players[: count // 2]
    trailing = [players[count - 1 - k_pos] for k_pos in range(count // 2)]
    return np.array(leading + trailing)


def reorder_table(count, turn):
    current = round_order(count, turn)
    following = round_order(count, (turn + 1) % (count - 1))
    where_now = np.zeros(count, dtype=np.int64)
    where_now[current] = np.arange(count)
    table = np.zeros((count, count), dtype=np.float32)
    table[where_now[following], np.arange(count)] = 1.0
    return table


def jacobi_sweep(joined, tables):
    count = joined.shape[1]
    half = count // 2
    for turn in range(count - 1):
        col_lead = joined[:, :half]
        col_trail = joined[:, half:]
        rot_lead = col_lead[:count]
        rot_trail = col_trail[:count]
        norm_lead = jnp.sum(rot_lead * rot_lead, axis=0)
        norm_trail = jnp.sum(rot_trail * rot_trail, axis=0)
        inner = jnp.sum(rot_lead * rot_trail, axis=0)
        contrast = norm_trail - norm_lead
        orient = jnp.where(contrast >= 0.0, 1.0, -1.0)
        denominator = jnp.abs(contrast) + jnp.sqrt(contrast * contrast + 4.0 * inner * inner)
        positive = denominator > 0.0
        tangent = jnp.where(
            positive, 2.0 * inner * orient / jnp.where(positive, denominator, 1.0), 0.0
        )
        cosine = 1.0 / jnp.sqrt(1.0 + tangent * tangent)
        sine_part = cosine * tangent
        rotated_pairs = jnp.concatenate(
            [cosine * col_lead - sine_part * col_trail, sine_part * col_lead + cosine * col_trail],
            axis=1,
        )
        joined = jnp.dot(
            rotated_pairs,
            tables[turn],
            precision=lax.Precision.HIGHEST,
            preferred_element_type=jnp.float32,
        )
    return joined


def jacobi(upper):
    count = upper.shape[1]
    start_order = round_order(count, 0)
    back_order = np.zeros(count, dtype=np.int64)
    back_order[start_order] = np.arange(count)
    tables = [jnp.asarray(reorder_table(count, turn)) for turn in range(count - 1)]
    joined = jnp.concatenate([upper, jnp.eye(count, dtype=jnp.float32)], axis=0)[:, start_order]
    joined = lax.fori_loop(
        0, SWEEPS, lambda sweep_index, state: jacobi_sweep(state, tables), joined
    )
    joined = joined[:, back_order]
    return (joined[:count], joined[count:])


def row_products(matrix):
    return lax.dot_general(
        matrix,
        matrix,
        (((1,), (1,)), ((), ())),
        precision=lax.Precision.HIGHEST,
        preferred_element_type=jnp.float32,
    )


def per_device(velocity, basis, levels, profile_index, advect):
    viscosity, face_down, face_up = profile(levels, profile_index)
    first = advance(with_faces(velocity), viscosity, face_down, face_up, advect)
    second = advance(with_faces(first), viscosity, face_down, face_up, advect)
    snapshots = jnp.stack([coarsen(first), coarsen(second)])
    own_rows = jnp.concatenate(
        [snapshots, lax.all_to_all(basis, "mode", split_axis=1, concat_axis=0, tiled=True)], axis=0
    )
    gram = row_products(own_rows)
    lower = jnp.linalg.cholesky(lax.psum(gram, ("space", "mode")))
    rotated, right_vecs = jacobi(lower.T)
    kept = rotated[:, :MODES]
    sigma = jnp.sqrt(jnp.sum(kept * kept, axis=0))
    updated = jnp.dot(
        right_vecs[:, :MODES].T,
        own_rows,
        precision=lax.Precision.HIGHEST,
        preferred_element_type=jnp.float32,
    )
    modes = lax.all_to_all(updated, "mode", split_axis=0, concat_axis=1, tiled=True)
    return (modes, sigma)


def solution(mesh):
    return jax.shard_map(
        per_device,
        mesh=mesh,
        in_specs=(P(None, "space", "mode", None), P("mode", "space"), P(), P(), P()),
        out_specs=(P("mode", "space"), P()),
        check_vma=False,
    )
```

profile of v0, /device:TPU:0, one launch (start us, length us, event | category | flops | bytes accessed | tf_op | source)
XLA Modules:
  0.0 329.9 jit_solution(12529537403124820518)
XLA Ops:
  0.7 2.1 fusion.664
  2.7 6.0 %collective-permute-start = (f32[3,1,128,256]{3,2,1,0:T(8,128)}, f32[3,1,128,256]{3,2,1,0:T(8,128)}, u32[]{:S(2)}, u32[]{:S(2)}) collective-permute-start(f32[3,1,128,256]{3,2,1,0:T(8,128)} %get-tuple-element.437), channel_id=1, source_target_pairs={{4,0},{8,4},{12,8},{16,12},{20,16},{24,20},{28,24},{32,28},{36,32}... | collective-permute-start | bytes 1179656 | tf_op jit(solution)/shard_map/ppermute | solution.py:21
  8.8 4.3 %all-to-all-start = ((f32[8,4,24576]{2,0,1:T(8,128)}), f32[8,4,24576]{2,0,1:T(8,128)S(1)}, u32[]{:S(2)}, u32[]{:S(2)}) async-start(f32[8,4,24576]{2,0,1:T(8,128)} %bitcast.223), calls=%async_computation | async-start | bytes 6291456 | tf_op jit(solution)/shard_map/all_to_all | solution.py:157
  15.0 2.0 pad_maximum_fusion.19
  17.1 3.9 %constant_dynamic-update-slice_fusion.1 = f32[3,18,128,256]{3,2,1,0:T(8,128)S(1)} fusion(f32[3,18,128,256]{3,2,1,0:T(8,128)S(1)} %constant_dynamic-update-slice_fusion.2, f32[3,16,128,256]{3,2,1,0:T(8,128)} %param.44), kind=kLoop, calls=%fused_computation.1005 | loop fusion | bytes 12582912
  22.1 2.9 copy-done.1
  25.7 3.2 collective-permute-start.2
  29.5 16.9 %collective-permute-done.2 = f32[3,18,1,256]{3,2,1,0:T(1,128)} collective-permute-done((f32[3,18,1,256]{3,2,1,0:T(1,128)}, f32[3,18,1,256]{3,2,1,0:T(1,128)}, u32[]{:S(2)}, u32[]{:S(2)}) %collective-permute-start.2) | collective-permute-done | bytes 55328 | tf_op jit(solution)/shard_map/ppermute | solution.py:21
  47.6 19.5 %fusion.631 = f32[3,16,128,256]{3,2,1,0:T(8,128)S(1)} fusion(f32[3,16,128,256]{3,2,1,0:T(8,128)} %param.44, f32[3,18,128,256]{3,2,1,0:T(8,128)} %copy-done.1, f32[3,18,1,256]{3,2,1,0:T(1,128)} %collective-permute-done.3, f32[3,18,1,256]{3,2,1,0:T(1,128)} %collective-permute-done.2, f32[3,1,128,256]{3,2,1,0:T(8,128)} %collective-permute-done, ...), kind=kLoop, calls=%fused_computation.935 | loop fusion | flops 31457280 | bytes 20561920 | tf_op jit(solution)/shard_map/sub | solution.py:48
  67.1 2.7 copy-done
  70.8 6.2 %reshape.1127 = f32[12,131072]{1,0:T(8,128)} reshape(f32[3,16,128,256]{3,2,1,0:T(8,128)} %copy-done) | data formatting | bytes 12582912 | tf_op jit(solution)/shard_map/reshape | solution.py:54
  78.2 5.2 %slice_add_fusion.3 = f32[12,32768]{1,0:T(8,128)} fusion(f32[12,131072]{1,0:T(8,128)} %reshape.1127), kind=kLoop, calls=%fused_computation.972 | loop fusion | flops 1179648 | bytes 7864320 | tf_op jit(solution)/shard_map/add | solution.py:57
  83.3 2.6 reshape.1128
  86.0 3.0 collective-permute-done.5
  89.0 1.9 pad_maximum_fusion.17
  90.8 2.1 collective-permute-start.6
  93.0 2.4 convolution_multiply_fusion.1
  95.4 1.7 copy.54
  97.1 1.7 stack_reshape.6
  98.8 22.4 %fusion.638 = f32[3,16,128,256]{3,2,1,0:T(8,128)} fusion(f32[3,16,128,256]{3,2,1,0:T(8,128)} %copy-done, f32[3,18,1,256]{3,2,1,0:T(1,128)} %collective-permute-done.7, f32[3,1,128,256]{3,2,1,0:T(8,128)S(1)} %collective-permute-done.4, f32[3,1,128,256]{3,2,1,0:T(8,128)} %collective-permute-done.5, f32[3,18,1,256]{3,2,1,0:T(1,128)} %collective-permute-done.6, ...), kind=kLoop, calls=%fused_computation.942 | loop fusion | flops 37748736 | bytes 13484032 | tf_op jit(solution)/shard_map/sub | solution.py:48
  121.2 6.2 %reshape.1129 = f32[12,131072]{1,0:T(8,128)} reshape(f32[3,16,128,256]{3,2,1,0:T(8,128)} %fusion.638) | data formatting | bytes 12582912 | tf_op jit(solution)/shard_map/reshape | solution.py:54
  127.4 5.2 %slice_add_fusion = f32[12,32768]{1,0:T(8,128)} fusion(f32[12,131072]{1,0:T(8,128)} %reshape.1129), kind=kLoop, calls=%fused_computation.969 | loop fusion | flops 1179648 | bytes 7864320 | tf_op jit(solution)/shard_map/add | solution.py:57
  132.6 2.6 reshape.1130
  135.2 1.8 convolution_multiply_fusion
  137.3 3.4 %fusion.651 = f32[34,34]{0,1:T(8,128)S(1)} fusion(f32[32,24576]{1,0:T(8,128)S(1)} %bitcast.219, f32[1,24576]{1,0:T(1,128)S(1)} %stack_reshape.7, f32[1,24576]{1,0:T(1,128)S(1)} %copy-done.2), kind=kOutput, calls=%fused_computation.968 | convolution fusion | flops 342589440 | bytes 3346960 | tf_op jit(solution)/shard_map/dot_general | solution.py:142
  140.8 65.2 %psum.7 = f32[34,34]{0,1:T(8,128)S(1)} all-reduce(f32[34,34]{0,1:T(8,128)S(1)} %fusion.651), channel_id=1, replica_groups=mesh['space'=32,'mode'=4] {'space','mode'}, use_global_device_ids=true, to_apply=%region_1.2 | all-reduce | flops 1156 | bytes 9248 | tf_op jit(solution)/shard_map/psum | solution.py:160
  206.0 3.1 cholesky.20
  212.2 69.3 %while.12 = (s32[]{:T(128)}, f32[68,34]{0,1:T(8,128)S(1)}, s32[]{:T(128)}, f32[17,34]{1,0:T(8,128)S(1)}, f32[17,34]{1,0:T(8,128)}) while((s32[]{:T(128)}, f32[68,34]{0,1:T(8,128)S(1)}, s32[]{:T(128)}, f32[17,34]{1,0:T(8,128)S(1)}, f32[17,34]{1,0:T(8,128)}) %tuple.273), condition=%wide.region_104.105_spmd.clone.clone, body=%wide.region_4.104_spmd.sunk.clone.clone.sunk | while | flops 31557920 | bytes 3821545 | solution.py:134
  282.2 4.7 %convolution_bitcast_fusion = f32[4,8,24576]{2,1,0:T(8,128)} fusion(f32[32,24576]{1,0:T(8,128)S(1)} %bitcast.220, f32[1,24576]{1,0:T(1,128)S(1)} %stack_reshape.7, f32[1,24576]{1,0:T(1,128)S(1)} %copy-done.2, f32[68,34]{0,1:T(8,128)S(1)} %bitcast.224), kind=kOutput, calls=%fused_computation.926 | convolution fusion | flops 322535424 | bytes 6504448 | tf_op jit(solution)/shard_map/dot_general | solution.py:164
  287.0 3.7 %all-to-all-start.1 = ((f32[4,8,24576]{2,1,0:T(8,128)}), f32[4,8,24576]{2,1,0:T(8,128)S(1)}, u32[]{:S(2)}, u32[]{:S(2)}) async-start(f32[4,8,24576]{2,1,0:T(8,128)} %convolution_bitcast_fusion), calls=%async_computation.1 | async-start | bytes 6291456 | tf_op jit(solution)/shard_map/all_to_all | solution.py:170
  291.3 36.9 %all-to-all-done.1 = f32[4,8,24576]{2,1,0:T(8,128)S(1)} async-done(((f32[4,8,24576]{2,1,0:T(8,128)}), f32[4,8,24576]{2,1,0:T(8,128)S(1)}, u32[]{:S(2)}, u32[]{:S(2)}) %all-to-all-start.1) | async-done | bytes 3145760 | tf_op jit(solution)/shard_map/all_to_all | solution.py:170
  328.2 1.7 copy.77
  (385 shorter events, 80.0 us)
Async XLA Ops:
  0.6 13.7 %copy-start.5 = (s32[34]{0:T(128)S(1)}, s32[34]{0:T(128)}, u32[]{:S(2)}) copy-start(s32[34]{0:T(128)} %constant.168) | copy-start | bytes 412
  0.6 13.1 %copy-start.4 = (f32[8]{0:T(128)S(1)}, f32[8]{0:T(128)}, u32[]{:S(2)}) copy-start(f32[8]{0:T(128)} %param.46) | copy-start | bytes 100
  0.7 13.0 %copy-start.3 = (s32[256]{0:T(256)S(1)}, s32[256]{0:T(256)}, u32[]{:S(2)}) copy-start(s32[256]{0:T(256)} %param.47) | copy-start | bytes 3076
  2.7 14.3 %collective-permute-start.1 = (f32[3,1,128,256]{3,2,1,0:T(8,128)}, f32[3,1,128,256]{3,2,1,0:T(8,128)S(1)}, u32[]{:S(2)}, u32[]{:S(2)}) collective-permute-start(f32[3,1,128,256]{3,2,1,0:T(8,128)} %get-tuple-element.438), channel_id=1, source_target_pairs={{0,4},{4,8},{8,12},{12,16},{16,20},{20,24},{24,28},{28,32},{32,36}... | collective-permute-start | bytes 1179656 | tf_op jit(solution)/shard_map/ppermute | solution.py:20
  2.7 18.3 %collective-permute-start = (f32[3,1,128,256]{3,2,1,0:T(8,128)}, f32[3,1,128,256]{3,2,1,0:T(8,128)}, u32[]{:S(2)}, u32[]{:S(2)}) collective-permute-start(f32[3,1,128,256]{3,2,1,0:T(8,128)} %get-tuple-element.437), channel_id=1, source_target_pairs={{4,0},{8,4},{12,8},{16,12},{20,16},{24,20},{28,24},{32,28},{36,32}... | collective-permute-start | bytes 1179656 | tf_op jit(solution)/shard_map/ppermute | solution.py:21
  8.8 128.5 %all-to-all-start = ((f32[8,4,24576]{2,0,1:T(8,128)}), f32[8,4,24576]{2,0,1:T(8,128)S(1)}, u32[]{:S(2)}, u32[]{:S(2)}) async-start(f32[8,4,24576]{2,0,1:T(8,128)} %bitcast.223), calls=%async_computation | async-start | bytes 6291456 | tf_op jit(solution)/shard_map/all_to_all | solution.py:157
  22.0 2.9 copy-start.1
  25.7 20.7 %collective-permute-start.2 = (f32[3,18,1,256]{3,2,1,0:T(1,128)}, f32[3,18,1,256]{3,2,1,0:T(1,128)}, u32[]{:S(2)}, u32[]{:S(2)}) collective-permute-start(f32[3,18,1,256]{3,2,1,0:T(1,128)} %get-tuple-element.433), channel_id=1, source_target_pairs={{1,0},{2,1},{3,2},{0,3},{5,4},{6,5},{7,6},{4,7},{9,8},{10,9},{11,1... | collective-permute-start | bytes 165896 | tf_op jit(solution)/shard_map/ppermute | solution.py:21
  28.9 18.7 %collective-permute-start.3 = (f32[3,18,1,256]{3,2,1,0:T(1,128)}, f32[3,18,1,256]{3,2,1,0:T(1,128)}, u32[]{:S(2)}, u32[]{:S(2)}) collective-permute-start(f32[3,18,1,256]{3,2,1,0:T(1,128)} %get-tuple-element.434), channel_id=1, source_target_pairs={{0,1},{1,2},{2,3},{3,0},{4,5},{5,6},{6,7},{7,4},{8,9},{9,10},{10,1... | collective-permute-start | bytes 165896 | tf_op jit(solution)/shard_map/ppermute | solution.py:20
  67.1 2.7 copy-start
  76.9 9.0 %collective-permute-start.4 = (f32[3,1,128,256]{3,2,1,0:T(8,128)}, f32[3,1,128,256]{3,2,1,0:T(8,128)S(1)}, u32[]{:S(2)}, u32[]{:S(2)}) collective-permute-start(f32[3,1,128,256]{3,2,1,0:T(8,128)} %get-tuple-element.436), channel_id=1, source_target_pairs={{4,0},{8,4},{12,8},{16,12},{20,16},{24,20},{28,24},{32,28},{36,32}... | collective-permute-start | bytes 1179656 | tf_op jit(solution)/shard_map/ppermute | solution.py:21
  78.2 10.8 %collective-permute-start.5 = (f32[3,1,128,256]{3,2,1,0:T(8,128)}, f32[3,1,128,256]{3,2,1,0:T(8,128)}, u32[]{:S(2)}, u32[]{:S(2)}) collective-permute-start(f32[3,1,128,256]{3,2,1,0:T(8,128)} %get-tuple-element.435), channel_id=1, source_target_pairs={{0,4},{4,8},{8,12},{12,16},{16,20},{20,24},{24,28},{28,32},{32,36}... | collective-permute-start | bytes 1179656 | tf_op jit(solution)/shard_map/ppermute | solution.py:20
  86.0 7.0 %copy-start.8 = (s32[256]{0:T(256)S(1)}, s32[256]{0:T(256)}, u32[]{:S(2)}) copy-start(s32[256]{0:T(256)} %and_select_fusion) | copy-start | bytes 3076
  90.8 7.9 %collective-permute-start.6 = (f32[3,18,1,256]{3,2,1,0:T(1,128)}, f32[3,18,1,256]{3,2,1,0:T(1,128)}, u32[]{:S(2)}, u32[]{:S(2)}) collective-permute-start(f32[3,18,1,256]{3,2,1,0:T(1,128)} %get-tuple-element.431), channel_id=1, source_target_pairs={{1,0},{2,1},{3,2},{0,3},{5,4},{6,5},{7,6},{4,7},{9,8},{10,9},{11,1... | collective-permute-start | bytes 165896 | tf_op jit(solution)/shard_map/ppermute | solution.py:21
  93.0 5.8 %collective-permute-start.7 = (f32[3,18,1,256]{3,2,1,0:T(1,128)}, f32[3,18,1,256]{3,2,1,0:T(1,128)}, u32[]{:S(2)}, u32[]{:S(2)}) collective-permute-start(f32[3,18,1,256]{3,2,1,0:T(1,128)} %get-tuple-element.432), channel_id=1, source_target_pairs={{0,1},{1,2},{2,3},{3,0},{4,5},{5,6},{6,7},{7,4},{8,9},{9,10},{10,1... | collective-permute-start | bytes 165896 | tf_op jit(solution)/shard_map/ppermute | solution.py:20
  127.4 7.8 %copy-start.9 = (s32[256]{0:T(256)S(1)}, s32[256]{0:T(256)}, u32[]{:S(2)}) copy-start(s32[256]{0:T(256)} %and_select_fusion) | copy-start | bytes 3076
  127.4 9.9 %copy-start.2 = (f32[1,24576]{1,0:T(1,128)S(1)}, f32[1,24576]{1,0:T(1,128)}, u32[]{:S(2)}) copy-start(f32[1,24576]{1,0:T(1,128)} %stack_reshape.6) | copy-start | bytes 294916
  132.6 79.6 %copy-start.6 = (f32[17,34]{1,0:T(8,128)S(1)}, f32[17,34]{1,0:T(8,128)}, u32[]{:S(2)}) copy-start(f32[17,34]{1,0:T(8,128)} %constant.970) | copy-start | bytes 6940
  212.2 21.9 %copy-start.7 = (f32[17,34]{1,0:T(8,128)S(1)}, f32[17,34]{1,0:T(8,128)}, u32[]{:S(2)}) copy-start(f32[17,34]{1,0:T(8,128)} %get-tuple-element.801) | copy-start | bytes 6940 | tf_op jit(solution)/shard_map/while
  246.7 22.0 %copy-start.7 = (f32[17,34]{1,0:T(8,128)S(1)}, f32[17,34]{1,0:T(8,128)}, u32[]{:S(2)}) copy-start(f32[17,34]{1,0:T(8,128)} %get-tuple-element.801) | copy-start | bytes 6940 | tf_op jit(solution)/shard_map/while
  287.0 41.3 %all-to-all-start.1 = ((f32[4,8,24576]{2,1,0:T(8,128)}), f32[4,8,24576]{2,1,0:T(8,128)S(1)}, u32[]{:S(2)}, u32[]{:S(2)}) async-start(f32[4,8,24576]{2,1,0:T(8,128)} %convolution_bitcast_fusion), calls=%async_computation.1 | async-start | bytes 6291456 | tf_op jit(solution)/shard_map/all_to_all | solution.py:170
where the time goes:
time: 333 us; the launch traced here: 330 us
  other arithmetic  75.4 us (23%)
  matrix products  68.1 us (20%)
  blocking collectives  65.2 us (20%)
  waiting for transfers between devices  58.1 us (17%)
  local copies, waits for them, and re-layouts  40 us (12%)
  starting transfers between devices  20.6 us (6%)
    psum x1, blocking collectives, per_device(): lower = jnp.linalg.cholesky(lax.psum(gram, ('space', 'mode')))  65.2 us
    dot_general x132, matrix products, jacobi_sweep(): jnp.dot(rotated_pairs, tables[turn], precision=lax.Precision.HIGHEST, pre...  55.7 us
    sub x2, other arithmetic, advance(): center + viscosity * lateral + vertical - 0.5 * advect * (east - west)  42 us
    all_to_all x1, waiting for transfers between devices, per_device(): lax.all_to_all(updated, 'mode', split_axis=0, concat_axis=1, tiled=True)  36.9 us
    ppermute x4, waiting for transfers between devices, extended(): after = lax.ppermute(leading, axis, down)  16.9 us
    ppermute x4, starting transfers between devices, extended(): after = lax.ppermute(leading, axis, down)  12.6 us
    reshape x2, local copies, waits for them, and re-layouts, coarsen(): slabs = field.reshape(components * (x_cells // STRIDE), STRIDE * plane)  12.3 us
    unnamed x21, local copies, waits for them, and re-layouts  11.2 us
  transfers between devices with their start and end apart: 10, of which 4 were waited for; matrix products, arithmetic and copies ran while one was open for 28% of the time, Pallas kernels for 0%

commit v1 on v0

--- a/solution.py
+++ b/solution.py
@@ -157,7 +157,7 @@
         [snapshots, lax.all_to_all(basis, "mode", split_axis=1, concat_axis=0, tiled=True)], axis=0
     )
     gram = row_products(own_rows)
-    lower = jnp.linalg.cholesky(lax.psum(gram, ("space", "mode")))
+    lower = jnp.linalg.cholesky(jnp.sum(lax.all_gather(gram, ("space", "mode")), axis=0))
     rotated, right_vecs = jacobi(lower.T)
     kept = rotated[:, :MODES]
     sigma = jnp.sqrt(jnp.sum(kept * kept, axis=0))

time: 333 us -> 319 us (0.958)
  matrix products: 68.1 us -> 46.8 us
  blocking collectives: 65.2 us -> 73.3 us
    all_gather x0 -> x1, blocking collectives: none -> 73.3 us  [per_device(): lax.all_gather(gram, ('space', 'mode'))]
    psum x1 -> x0, blocking collectives: 65.2 us -> none  [per_device(): lower = jnp.linalg.cholesky(lax.psum(gram, ('space', 'mode')))]
    dot_general x132, matrix products: 55.7 us -> 34.5 us  [jacobi_sweep(): jnp.dot(rotated_pairs, tables[turn], precision=lax.Precision.HIGHEST, pre...]
    unnamed x21 -> x25, local copies, waits for them, and re-layouts: 11.2 us -> 11.2 us
  transfers between devices with their start and end apart: 10 -> 10, of which waited for: 4 -> 4; matrix products, arithmetic and copies ran while one was open for 28% -> 29% of each run, Pallas kernels for 0% -> 0%
where the time goes in v1:
time: 319 us; the launch traced here: 318 us
  other arithmetic  76.7 us (24%)
  blocking collectives  73.3 us (23%)
  waiting for transfers between devices  58 us (18%)
  matrix products  46.8 us (15%)
  local copies, waits for them, and re-layouts  40 us (13%)
  starting transfers between devices  20.6 us (6%)
    all_gather x1, blocking collectives, per_device(): lax.all_gather(gram, ('space', 'mode'))  73.3 us
    sub x2, other arithmetic, advance(): center + viscosity * lateral + vertical - 0.5 * advect * (east - west)  42 us
    all_to_all x1, waiting for transfers between devices, per_device(): lax.all_to_all(updated, 'mode', split_axis=0, concat_axis=1, tiled=True)  36.9 us
    dot_general x132, matrix products, jacobi_sweep(): jnp.dot(rotated_pairs, tables[turn], precision=lax.Precision.HIGHEST, pre...  34.5 us
    ppermute x4, waiting for transfers between devices, extended(): after = lax.ppermute(leading, axis, down)  16.9 us
    ppermute x4, starting transfers between devices, extended(): after = lax.ppermute(leading, axis, down)  12.6 us
    reshape x2, local copies, waits for them, and re-layouts, coarsen(): slabs = field.reshape(components * (x_cells // STRIDE), STRIDE * plane)  12.3 us
    unnamed x25, local copies, waits for them, and re-layouts  11.2 us
  transfers between devices with their start and end apart: 10, of which 4 were waited for; matrix products, arithmetic and copies ran while one was open for 29% of the time, Pallas kernels for 0%

profile of v1, /device:TPU:0, one launch (start us, length us, event | category | flops | bytes accessed | tf_op | source)
XLA Modules:
  0.0 318.0 jit_solution(14433965005957070191)
XLA Ops:
  0.7 2.1 fusion.665
  2.7 6.0 %collective-permute-start = (f32[3,1,128,256]{3,2,1,0:T(8,128)}, f32[3,1,128,256]{3,2,1,0:T(8,128)}, u32[]{:S(2)}, u32[]{:S(2)}) collective-permute-start(f32[3,1,128,256]{3,2,1,0:T(8,128)} %get-tuple-element.437), channel_id=1, source_target_pairs={{4,0},{8,4},{12,8},{16,12},{20,16},{24,20},{28,24},{32,28},{36,32}... | collective-permute-start | bytes 1179656 | tf_op jit(solution)/shard_map/ppermute | solution.py:21
  8.8 4.3 %all-to-all-start = ((f32[8,4,24576]{2,0,1:T(8,128)}), f32[8,4,24576]{2,0,1:T(8,128)S(1)}, u32[]{:S(2)}, u32[]{:S(2)}) async-start(f32[8,4,24576]{2,0,1:T(8,128)} %bitcast.225), calls=%async_computation | async-start | bytes 6291456 | tf_op jit(solution)/shard_map/all_to_all | solution.py:157
  15.0 2.0 pad_maximum_fusion.21
  17.1 3.9 %constant_dynamic-update-slice_fusion.1 = f32[3,18,128,256]{3,2,1,0:T(8,128)S(1)} fusion(f32[3,18,128,256]{3,2,1,0:T(8,128)S(1)} %constant_dynamic-update-slice_fusion.2, f32[3,16,128,256]{3,2,1,0:T(8,128)} %param.44), kind=kLoop, calls=%fused_computation.1006 | loop fusion | bytes 12582912
  22.1 2.9 copy-done.1
  25.7 3.2 %collective-permute-start.2 = (f32[3,18,1,256]{3,2,1,0:T(1,128)}, f32[3,18,1,256]{3,2,1,0:T(1,128)}, u32[]{:S(2)}, u32[]{:S(2)}) collective-permute-start(f32[3,18,1,256]{3,2,1,0:T(1,128)} %get-tuple-element.433), channel_id=1, source_target_pairs={{1,0},{2,1},{3,2},{0,3},{5,4},{6,5},{7,6},{4,7},{9,8},{10,9},{11,1... | collective-permute-start | bytes 165896 | tf_op jit(solution)/shard_map/ppermute | solution.py:21
  29.5 16.9 %collective-permute-done.2 = f32[3,18,1,256]{3,2,1,0:T(1,128)} collective-permute-done((f32[3,18,1,256]{3,2,1,0:T(1,128)}, f32[3,18,1,256]{3,2,1,0:T(1,128)}, u32[]{:S(2)}, u32[]{:S(2)}) %collective-permute-start.2) | collective-permute-done | bytes 55328 | tf_op jit(solution)/shard_map/ppermute | solution.py:21
  47.6 19.5 %fusion.631 = f32[3,16,128,256]{3,2,1,0:T(8,128)S(1)} fusion(f32[3,16,128,256]{3,2,1,0:T(8,128)} %param.44, f32[3,18,128,256]{3,2,1,0:T(8,128)} %copy-done.1, f32[3,18,1,256]{3,2,1,0:T(1,128)} %collective-permute-done.3, f32[3,18,1,256]{3,2,1,0:T(1,128)} %collective-permute-done.2, f32[3,1,128,256]{3,2,1,0:T(8,128)} %collective-permute-done, ...), kind=kLoop, calls=%fused_computation.935 | loop fusion | flops 31457280 | bytes 20561920 | tf_op jit(solution)/shard_map/sub | solution.py:48
  67.1 2.7 copy-done
  70.8 6.2 %reshape.1127 = f32[12,131072]{1,0:T(8,128)} reshape(f32[3,16,128,256]{3,2,1,0:T(8,128)} %copy-done) | data formatting | bytes 12582912 | tf_op jit(solution)/shard_map/reshape | solution.py:54
  78.2 5.2 %slice_add_fusion.3 = f32[12,32768]{1,0:T(8,128)} fusion(f32[12,131072]{1,0:T(8,128)} %reshape.1127), kind=kLoop, calls=%fused_computation.972 | loop fusion | flops 1179648 | bytes 7864320 | tf_op jit(solution)/shard_map/add | solution.py:57
  83.3 2.6 reshape.1128
  86.0 3.0 collective-permute-done.5
  89.0 1.9 pad_maximum_fusion.19
  90.8 2.1 collective-permute-start.6
  93.0 2.4 convolution_multiply_fusion.1
  95.4 1.7 copy.57
  97.1 1.7 stack_reshape.6
  98.8 22.4 %fusion.638 = f32[3,16,128,256]{3,2,1,0:T(8,128)} fusion(f32[3,16,128,256]{3,2,1,0:T(8,128)} %copy-done, f32[3,18,1,256]{3,2,1,0:T(1,128)} %collective-permute-done.7, f32[3,1,128,256]{3,2,1,0:T(8,128)S(1)} %collective-permute-done.4, f32[3,1,128,256]{3,2,1,0:T(8,128)} %collective-permute-done.5, f32[3,18,1,256]{3,2,1,0:T(1,128)} %collective-permute-done.6, ...), kind=kLoop, calls=%fused_computation.942 | loop fusion | flops 37748736 | bytes 13484032 | tf_op jit(solution)/shard_map/sub | solution.py:48
  121.2 6.2 %reshape.1129 = f32[12,131072]{1,0:T(8,128)} reshape(f32[3,16,128,256]{3,2,1,0:T(8,128)} %fusion.638) | data formatting | bytes 12582912 | tf_op jit(solution)/shard_map/reshape | solution.py:54
  127.4 5.2 %slice_add_fusion = f32[12,32768]{1,0:T(8,128)} fusion(f32[12,131072]{1,0:T(8,128)} %reshape.1129), kind=kLoop, calls=%fused_computation.969 | loop fusion | flops 1179648 | bytes 7864320 | tf_op jit(solution)/shard_map/add | solution.py:57
  132.6 2.6 reshape.1130
  135.2 1.8 convolution_multiply_fusion
  137.3 3.4 %fusion.652 = f32[1,34,34]{2,1,0:T(8,128)S(1)} fusion(f32[32,24576]{1,0:T(8,128)S(1)} %bitcast.221, f32[1,24576]{1,0:T(1,128)S(1)} %stack_reshape.7, f32[1,24576]{1,0:T(1,128)S(1)} %copy-done.2), kind=kOutput, calls=%fused_computation.977 | convolution fusion | flops 342589440 | bytes 3346960 | tf_op jit(solution)/shard_map/dot_general | solution.py:142
  140.8 73.3 %all-gather.1 = f32[128,34,34]{2,1,0:T(8,128)} all-gather(f32[1,34,34]{2,1,0:T(8,128)S(1)} %fusion.652), channel_id=2, replica_groups=mesh['space'=32,'mode'=4] {'space','mode'}, dimensions={0}, use_global_device_ids=true | all-gather | bytes 596496 | tf_op jit(solution)/shard_map/all_gather | solution.py:160
  214.1 2.0 reduce_sum.919
  216.2 3.1 cholesky.20
  221.6 48.1 %while.12 = (s32[]{:T(128)}, f32[68,34]{0,1:T(8,128)S(1)}, s32[]{:T(128)}, f32[17,34]{1,0:T(8,128)S(1)}, f32[17,34]{1,0:T(8,128)S(1)}) while((s32[]{:T(128)}, f32[68,34]{0,1:T(8,128)S(1)}, s32[]{:T(128)}, f32[17,34]{1,0:T(8,128)S(1)}, f32[17,34]{1,0:T(8,128)S(1)}) %tuple.274), condition=%wide.region_104.105_spmd.clone.clone, body=%wide.region_4.104_spmd.sunk.clone.clone.sunk | while | flops 31557920 | bytes 3961909 | solution.py:134
  270.4 4.7 %convolution_bitcast_fusion = f32[4,8,24576]{2,1,0:T(8,128)} fusion(f32[32,24576]{1,0:T(8,128)S(1)} %bitcast.222, f32[1,24576]{1,0:T(1,128)S(1)} %stack_reshape.7, f32[1,24576]{1,0:T(1,128)S(1)} %copy-done.2, f32[68,34]{0,1:T(8,128)S(1)} %bitcast.226), kind=kOutput, calls=%fused_computation.926 | convolution fusion | flops 322535424 | bytes 6504448 | tf_op jit(solution)/shard_map/dot_general | solution.py:164
  275.1 3.7 %all-to-all-start.1 = ((f32[4,8,24576]{2,1,0:T(8,128)}), f32[4,8,24576]{2,1,0:T(8,128)S(1)}, u32[]{:S(2)}, u32[]{:S(2)}) async-start(f32[4,8,24576]{2,1,0:T(8,128)} %convolution_bitcast_fusion), calls=%async_computation.1 | async-start | bytes 6291456 | tf_op jit(solution)/shard_map/all_to_all | solution.py:170
  279.5 36.9 %all-to-all-done.1 = f32[4,8,24576]{2,1,0:T(8,128)S(1)} async-done(((f32[4,8,24576]{2,1,0:T(8,128)}), f32[4,8,24576]{2,1,0:T(8,128)S(1)}, u32[]{:S(2)}, u32[]{:S(2)}) %all-to-all-start.1) | async-done | bytes 3145760 | tf_op jit(solution)/shard_map/all_to_all | solution.py:170
  (386 shorter events, 59.8 us)
Async XLA Ops:
  0.6 13.7 %copy-start.6 = (s32[34]{0:T(128)S(1)}, s32[34]{0:T(128)}, u32[]{:S(2)}) copy-start(s32[34]{0:T(128)} %constant.168) | copy-start | bytes 412
  0.6 13.1 %copy-start.5 = (f32[8]{0:T(128)S(1)}, f32[8]{0:T(128)}, u32[]{:S(2)}) copy-start(f32[8]{0:T(128)} %param.46) | copy-start | bytes 100
  0.7 13.0 %copy-start.4 = (s32[256]{0:T(256)S(1)}, s32[256]{0:T(256)}, u32[]{:S(2)}) copy-start(s32[256]{0:T(256)} %param.47) | copy-start | bytes 3076
  2.7 14.3 %collective-permute-start.1 = (f32[3,1,128,256]{3,2,1,0:T(8,128)}, f32[3,1,128,256]{3,2,1,0:T(8,128)S(1)}, u32[]{:S(2)}, u32[]{:S(2)}) collective-permute-start(f32[3,1,128,256]{3,2,1,0:T(8,128)} %get-tuple-element.438), channel_id=1, source_target_pairs={{0,4},{4,8},{8,12},{12,16},{16,20},{20,24},{24,28},{28,32},{32,36}... | collective-permute-start | bytes 1179656 | tf_op jit(solution)/shard_map/ppermute | solution.py:20
  2.7 18.3 %collective-permute-start = (f32[3,1,128,256]{3,2,1,0:T(8,128)}, f32[3,1,128,256]{3,2,1,0:T(8,128)}, u32[]{:S(2)}, u32[]{:S(2)}) collective-permute-start(f32[3,1,128,256]{3,2,1,0:T(8,128)} %get-tuple-element.437), channel_id=1, source_target_pairs={{4,0},{8,4},{12,8},{16,12},{20,16},{24,20},{28,24},{32,28},{36,32}... | collective-permute-start | bytes 1179656 | tf_op jit(solution)/shard_map/ppermute | solution.py:21
  8.8 128.5 %all-to-all-start = ((f32[8,4,24576]{2,0,1:T(8,128)}), f32[8,4,24576]{2,0,1:T(8,128)S(1)}, u32[]{:S(2)}, u32[]{:S(2)}) async-start(f32[8,4,24576]{2,0,1:T(8,128)} %bitcast.225), calls=%async_computation | async-start | bytes 6291456 | tf_op jit(solution)/shard_map/all_to_all | solution.py:157
  22.0 2.9 copy-start.1
  25.7 20.7 %collective-permute-start.2 = (f32[3,18,1,256]{3,2,1,0:T(1,128)}, f32[3,18,1,256]{3,2,1,0:T(1,128)}, u32[]{:S(2)}, u32[]{:S(2)}) collective-permute-start(f32[3,18,1,256]{3,2,1,0:T(1,128)} %get-tuple-element.433), channel_id=1, source_target_pairs={{1,0},{2,1},{3,2},{0,3},{5,4},{6,5},{7,6},{4,7},{9,8},{10,9},{11,1... | collective-permute-start | bytes 165896 | tf_op jit(solution)/shard_map/ppermute | solution.py:21
  28.9 18.7 %collective-permute-start.3 = (f32[3,18,1,256]{3,2,1,0:T(1,128)}, f32[3,18,1,256]{3,2,1,0:T(1,128)}, u32[]{:S(2)}, u32[]{:S(2)}) collective-permute-start(f32[3,18,1,256]{3,2,1,0:T(1,128)} %get-tuple-element.434), channel_id=1, source_target_pairs={{0,1},{1,2},{2,3},{3,0},{4,5},{5,6},{6,7},{7,4},{8,9},{9,10},{10,1... | collective-permute-start | bytes 165896 | tf_op jit(solution)/shard_map/ppermute | solution.py:20
  67.1 2.7 copy-start
  76.9 9.0 %collective-permute-start.4 = (f32[3,1,128,256]{3,2,1,0:T(8,128)}, f32[3,1,128,256]{3,2,1,0:T(8,128)S(1)}, u32[]{:S(2)}, u32[]{:S(2)}) collective-permute-start(f32[3,1,128,256]{3,2,1,0:T(8,128)} %get-tuple-element.436), channel_id=1, source_target_pairs={{4,0},{8,4},{12,8},{16,12},{20,16},{24,20},{28,24},{32,28},{36,32}... | collective-permute-start | bytes 1179656 | tf_op jit(solution)/shard_map/ppermute | solution.py:21
  78.2 10.8 %collective-permute-start.5 = (f32[3,1,128,256]{3,2,1,0:T(8,128)}, f32[3,1,128,256]{3,2,1,0:T(8,128)}, u32[]{:S(2)}, u32[]{:S(2)}) collective-permute-start(f32[3,1,128,256]{3,2,1,0:T(8,128)} %get-tuple-element.435), channel_id=1, source_target_pairs={{0,4},{4,8},{8,12},{12,16},{16,20},{20,24},{24,28},{28,32},{32,36}... | collective-permute-start | bytes 1179656 | tf_op jit(solution)/shard_map/ppermute | solution.py:20
  86.0 7.0 %copy-start.9 = (s32[256]{0:T(256)S(1)}, s32[256]{0:T(256)}, u32[]{:S(2)}) copy-start(s32[256]{0:T(256)} %and_select_fusion) | copy-start | bytes 3076
  90.8 7.9 %collective-permute-start.6 = (f32[3,18,1,256]{3,2,1,0:T(1,128)}, f32[3,18,1,256]{3,2,1,0:T(1,128)}, u32[]{:S(2)}, u32[]{:S(2)}) collective-permute-start(f32[3,18,1,256]{3,2,1,0:T(1,128)} %get-tuple-element.431), channel_id=1, source_target_pairs={{1,0},{2,1},{3,2},{0,3},{5,4},{6,5},{7,6},{4,7},{9,8},{10,9},{11,1... | collective-permute-start | bytes 165896 | tf_op jit(solution)/shard_map/ppermute | solution.py:21
  93.0 5.8 %collective-permute-start.7 = (f32[3,18,1,256]{3,2,1,0:T(1,128)}, f32[3,18,1,256]{3,2,1,0:T(1,128)}, u32[]{:S(2)}, u32[]{:S(2)}) collective-permute-start(f32[3,18,1,256]{3,2,1,0:T(1,128)} %get-tuple-element.432), channel_id=1, source_target_pairs={{0,1},{1,2},{2,3},{3,0},{4,5},{5,6},{6,7},{7,4},{8,9},{9,10},{10,1... | collective-permute-start | bytes 165896 | tf_op jit(solution)/shard_map/ppermute | solution.py:20
  127.4 7.8 %copy-start.10 = (s32[256]{0:T(256)S(1)}, s32[256]{0:T(256)}, u32[]{:S(2)}) copy-start(s32[256]{0:T(256)} %and_select_fusion) | copy-start | bytes 3076
  127.4 10.0 %copy-start.2 = (f32[1,24576]{1,0:T(1,128)S(1)}, f32[1,24576]{1,0:T(1,128)}, u32[]{:S(2)}) copy-start(f32[1,24576]{1,0:T(1,128)} %stack_reshape.6) | copy-start | bytes 294916
  135.2 86.4 %copy-start.7 = (f32[17,34]{1,0:T(8,128)S(1)}, f32[17,34]{1,0:T(8,128)}, u32[]{:S(2)}) copy-start(f32[17,34]{1,0:T(8,128)} %constant.971) | copy-start | bytes 6940
  137.3 83.5 %copy-start.3 = (f32[34,34]{0,1:T(8,128)S(1)}, f32[34,34]{0,1:T(8,128)}, u32[]{:S(2)}) copy-start(f32[34,34]{0,1:T(8,128)} %fusion.658) | copy-start | bytes 13876
  137.3 84.3 %copy-start.8 = (f32[17,34]{1,0:T(8,128)S(1)}, f32[17,34]{1,0:T(8,128)}, u32[]{:S(2)}) copy-start(f32[17,34]{1,0:T(8,128)} %constant.972) | copy-start | bytes 6940
  275.1 41.2 %all-to-all-start.1 = ((f32[4,8,24576]{2,1,0:T(8,128)}), f32[4,8,24576]{2,1,0:T(8,128)S(1)}, u32[]{:S(2)}, u32[]{:S(2)}) async-start(f32[4,8,24576]{2,1,0:T(8,128)} %convolution_bitcast_fusion), calls=%async_computation.1 | async-start | bytes 6291456 | tf_op jit(solution)/shard_map/all_to_all | solution.py:170
